TPU v7x, 32 devices: a whole 2x2x4 slice. The times are simulated.
32 devices in a mesh: obs: 4 (over x, core), ord: 8 (over z, y).
Axes of the slice: x: 2, y: 2, z: 4, core: 2. Of those that a mesh axis runs over, the one named last changes fastest.
Arguments:
- longitude: float32 [4, 32768], P('obs'), may hold values from -3.140625 to 3.140625
- cycle_of: int32 [4, 32768], P('obs'), may hold values from 0 to 255, never falling along the last dimension, each value on 1 to 256 neighbouring positions
- obs_count: int32 [4], P('obs'), may hold values from 16384 to 32768
- observed: float32 [4, 32768], P('obs'), may hold values from -896 to 896
- obs_weight: float32 [4, 32768], P('obs'), may hold values from 0.3 to 3
- legendre: float32 [4, 72, 288, 256], P('obs', 'ord'), as said below
- precond_inv: float32 [72, 288, 288], P('ord'), as said below
- order_of_slot: int32 [72], P('ord'), may hold values from 0 to 71, each once
Outputs:
- solution: float32 [72, 2, 288], P('ord')
- residual: float32 [72, 2, 288], P('ord')
Inputs may be any that keep to these rules, and one draw needn't show every extreme that they name: `cycle_of`: cycle numbers never fall along a slab; each cycle holds at least one observation slot. `obs_count`: observation slots at or beyond a slab's count carry no weight. legendre[b, m, n, j] is the fully normalized associated Legendre function of degree n and order m at the colatitude of cycle j of slab b, and 0 for n < m. `precond_inv`: every block is symmetric positive definite. order_of_slot names each order once; slot s lies on ord index s // 9.
All inputs are finite; a program needn't handle non-finite values.
Results may differ from a plain program's by a relative error of at most 0.0003.
Values sent between devices are 32-bit elements; how exact they have to be, the bound alone decides.
No kernel may reach another device: no remote copies, remote signals or barrier semaphores. Data moves between devices by JAX's collectives and lax.ppermute only.
A program may use at most 128 MiB of HBM per device.

v0:
```python
import math
import jax
import jax.numpy as jnp
from jax import lax
from jax.sharding import PartitionSpec as P

ITERS = 2
PRECISE = lax.Precision.HIGHEST


def block_split(cycle_ids):
    slab_size = cycle_ids.shape[0]
    block = math.gcd(slab_size, 4096)
    return (block, slab_size // block)


def spread_cycles(cycle_values, cycle_ids):
    rows = cycle_values.shape[0] * cycle_values.shape[1]
    cycle_count = cycle_values.shape[2]
    flat_cycles = cycle_values.reshape(rows, cycle_count)
    block, blocks = block_split(cycle_ids)
    cycle_iota = jnp.arange(cycle_count, dtype=jnp.int32)

    def one_block(id_block):
        onehot = (id_block[:, None] == cycle_iota[None, :]).astype(jnp.float32)
        return jnp.dot(onehot, flat_cycles.T, precision=PRECISE, preferred_element_type=jnp.float32)

    pieces = lax.map(one_block, cycle_ids.reshape(blocks, block))
    at_points = pieces.reshape(blocks * block, rows).T
    return at_points.reshape(cycle_values.shape[0], cycle_values.shape[1], blocks * block)


def collect_cycles(weighted, cycle_ids, cycle_count):
    lead = weighted.shape[0]
    pair = weighted.shape[1]
    rows = lead * pair
    block, blocks = block_split(cycle_ids)
    cycle_iota = jnp.arange(cycle_count, dtype=jnp.int32)
    flat = jnp.moveaxis(weighted.reshape(rows, blocks, block), 1, 0)

    def add_block(total, block_data):
        id_block, value_block = block_data
        onehot = (id_block[:, None] == cycle_iota[None, :]).astype(jnp.float32)
        return (
            total
            + jnp.dot(value_block, onehot, precision=PRECISE, preferred_element_type=jnp.float32),
            None,
        )

    total, unused = lax.scan(
        add_block,
        jnp.zeros((rows, cycle_count), jnp.float32),
        (cycle_ids.reshape(blocks, block), flat),
    )
    return total.reshape(lead, pair, cycle_count)


def synthesize(coefficients, legendre_here, harmonic, cycle_ids):
    cycle_values = jnp.einsum("okn,onr->okr", coefficients, legendre_here, precision=PRECISE)
    at_points = spread_cycles(cycle_values, cycle_ids)
    return jnp.sum(at_points * harmonic, axis=(0, 1))


def adjoint(values, legendre_here, harmonic, cycle_ids):
    weighted = harmonic * values[None, None, :]
    per_cycle = collect_cycles(weighted, cycle_ids, legendre_here.shape[2])
    return jnp.einsum("okr,onr->okn", per_cycle, legendre_here, precision=PRECISE)


def body(
    longitude, cycle_of, obs_count, observed, obs_weight, legendre, precond_inv, order_of_slot
):
    count_here = legendre.shape[1]
    degrees = legendre.shape[2]
    legendre_here = legendre[0]
    east = longitude[0]
    cycle_ids = cycle_of[0]
    slab_size = east.shape[0]
    positions = jnp.arange(slab_size, dtype=jnp.int32)
    total_obs = slab_size * lax.axis_size("obs")
    obs_scale = obs_weight[0] * (positions < obs_count[0]).astype(jnp.float32) / total_obs
    first_order = lax.axis_index("ord") * count_here
    block_orders = first_order + jnp.arange(count_here, dtype=jnp.int32)
    angles = block_orders.astype(jnp.float32)[:, None] * east[None, :]
    harmonic = jnp.stack([jnp.cos(angles), jnp.sin(angles)], axis=1)
    every_owner = lax.all_gather(order_of_slot, "ord", axis=0, tiled=True)
    slot_ids = jnp.arange(every_owner.shape[0], dtype=jnp.int32)
    slot_of_block = jnp.sum(
        jnp.where(every_owner[None, :] == block_orders[:, None], slot_ids[None, :], 0), axis=1
    )
    live_mask = (
        jnp.arange(degrees, dtype=jnp.int32)[None, None, :] >= order_of_slot[:, None, None]
    ).astype(jnp.float32)

    def owner_rows(partial_value):
        summed = lax.psum(partial_value, "obs")
        everyone = lax.all_gather(summed, "ord", axis=0, tiled=True)
        return jnp.take(everyone, order_of_slot, axis=0)

    def precondition(values):
        return live_mask * jnp.einsum("snj,skj->skn", precond_inv, values, precision=PRECISE)

    def energy(values, precond):
        return lax.psum(jnp.sum(values * precond), "ord")

    residual = owner_rows(adjoint(obs_scale * observed[0], legendre_here, harmonic, cycle_ids))
    solution = jnp.zeros_like(residual)
    precond = precondition(residual)
    direction = precond
    energy_now = energy(residual, precond)
    for iteration in range(ITERS):
        block_everyone = lax.all_gather(direction, "ord", axis=0, tiled=True)
        coefficients = jnp.take(block_everyone, slot_of_block, axis=0)
        gradient = lax.psum(synthesize(coefficients, legendre_here, harmonic, cycle_ids), "ord")
        weighted = obs_scale * gradient
        curvature_sum = lax.psum(jnp.sum(weighted * gradient), "obs")
        image = owner_rows(adjoint(weighted, legendre_here, harmonic, cycle_ids))
        image, curvature_sum = (image, curvature_sum)
        step_size = energy_now / curvature_sum
        solution = solution + step_size * direction
        residual = residual - step_size * image
        if iteration + 1 < ITERS:
            precond = precondition(residual)
            energy_next = energy(residual, precond)
            direction = precond + energy_next / energy_now * direction
            energy_now = energy_next
    return (solution, residual)


def solution(mesh):
    placed = (
        P("obs", None),
        P("obs", None),
        P("obs"),
        P("obs", None),
        P("obs", None),
        P("obs", "ord", None, None),
        P("ord", None, None),
        P("ord"),
    )
    return jax.shard_map(
        body,
        mesh=mesh,
        in_specs=placed,
        out_specs=(P("ord", None, None), P("ord", None, None)),
        check_vma=False,
    )
```

profile of v0, /device:TPU:0, one launch (start us, length us, event | category | flops | bytes accessed | tf_op | source)
XLA Modules:
  0.0 720.2 jit_solution(2464493801423855208)
XLA Ops:
  12.2 13.1 %all-reduce = s32[72]{0:T(128)S(1)} all-reduce(s32[72]{0:T(128)S(1)} %dynamic-update-slice), channel_id=1, replica_groups=mesh['obs'=4,'ord'=8] {'ord'}, use_global_device_ids=true, to_apply=%add | all-reduce | flops 72 | bytes 576
  25.5 33.9 %multiply_cosine_fusion = (f32[9,1,32768]{2,1,0:T(1,128)S(1)}, f32[9,1,32768]{2,1,0:T(1,128)S(1)}) fusion(f32[32768]{0:T(1024)} %bitcast.105, f32[9]{0:T(128)S(1)} %fusion.46), kind=kLoop, calls=%fused_computation.58 | loop fusion | flops 294912 | bytes 2490404 | tf_op jit(solution)/shard_map/cos | solution.py:85
  59.4 3.5 pad_maximum_fusion
  62.9 4.2 stack.10
  67.2 4.6 stack.11
  76.1 3.3 multiply_bitcast_fusion.2
  79.4 28.7 %while.57 = (s32[]{:T(128)}, f32[18,256]{1,0:T(8,128)S(1)}, f32[8,18,4096]{2,0,1:T(8,128)}, s32[8,4096]{1,0:T(8,128)S(1)}, s32[]{:T(128)}, /*index=5*/s32[]{:T(128)}) while((s32[]{:T(128)}, f32[18,256]{1,0:T(8,128)S(1)}, f32[8,18,4096]{2,0,1:T(8,128)}, s32[8,4096]{1,0:T(8,128)S(1)}, s32[]{:T(128)}, /*index=5*/s32[]{:T(128)}) %tuple.107), condition=%wide.region_1.2_spmd.clone, body=%wide.region_0.1_spmd.clone.sunk | while | flops 227550208 | bytes 970839 | solution.py:50
  108.1 2.3 fusion.31
  110.4 10.3 %psum.63 = f32[9,2,288]{2,1,0:T(2,128)S(1)} all-reduce(f32[9,2,288]{2,1,0:T(2,128)S(1)} %fusion.31), channel_id=1, replica_groups=mesh['obs'=4,'ord'=8] {'obs'}, use_global_device_ids=true, to_apply=%region_2.3 | all-reduce | flops 5184 | bytes 41472 | tf_op jit(solution)/shard_map/psum | solution.py:96
  120.7 30.7 %all_gather.18 = f32[72,2,288]{2,1,0:T(2,128)S(1)} all-gather(f32[9,2,288]{2,1,0:T(2,128)S(1)} %psum.63), channel_id=1, replica_groups=mesh['obs'=4,'ord'=8] {'ord'}, dimensions={0}, use_global_device_ids=true | all-gather | bytes 186624 | tf_op jit(solution)/shard_map/all_gather | solution.py:97
  152.0 6.2 multiply_reduce_fusion.3
  158.2 30.7 %all_gather.19 = f32[72,2,288]{2,1,0:T(2,128)S(1)} all-gather(f32[9,2,288]{2,1,0:T(2,128)S(1)} %get-tuple-element.301), channel_id=1, replica_groups=mesh['obs'=4,'ord'=8] {'ord'}, dimensions={0}, use_global_device_ids=true | all-gather | bytes 186624 | tf_op jit(solution)/shard_map/all_gather | solution.py:112
  192.6 75.7 %while.55 = (s32[]{:T(128)}, f32[8,4096,18]{1,0,2:T(8,128)}, s32[8,4096]{1,0:T(8,128)S(1)}, f32[18,256]{1,0:T(8,128)S(1)}, s32[]{:T(128)}, /*index=5*/s32[]{:T(128)}) while((s32[]{:T(128)}, f32[8,4096,18]{1,0,2:T(8,128)}, s32[8,4096]{1,0:T(8,128)S(1)}, f32[18,256]{1,0:T(8,128)S(1)}, s32[]{:T(128)}, /*index=5*/s32[]{:T(128)}) %tuple.126), condition=%wide.region_7.9_spmd.clone, body=%wide.region_6.8_spmd.clone.sunk | while | flops 227540992 | bytes 1542221 | solution.py:28
  192.6 2.6 convolution_bitcast_fusion.4
  195.5 6.6 dynamic_update_slice.11
  202.0 2.6 convolution_bitcast_fusion.4
  204.9 6.6 dynamic_update_slice.11
  211.5 2.6 convolution_bitcast_fusion.4
  214.4 6.6 dynamic_update_slice.11
  221.0 2.6 convolution_bitcast_fusion.4
  223.9 6.6 dynamic_update_slice.11
  230.4 2.6 convolution_bitcast_fusion.4
  233.3 6.6 dynamic_update_slice.11
  239.9 2.6 convolution_bitcast_fusion.4
  242.8 6.6 dynamic_update_slice.11
  249.4 2.6 convolution_bitcast_fusion.4
  252.2 6.6 dynamic_update_slice.11
  258.8 2.6 convolution_bitcast_fusion.4
  261.7 6.6 dynamic_update_slice.11
  268.3 2.0 pad.7
  273.5 19.6 %psum.64 = f32[]{:T(128)} all-reduce(f32[]{:T(128)} %get-tuple-element.300), channel_id=1, replica_groups=mesh['obs'=4,'ord'=8] {'ord'}, use_global_device_ids=true, to_apply=%region_4.6 | all-reduce | flops 1 | bytes 8 | tf_op jit(solution)/shard_map/psum | solution.py:104
  293.1 49.5 %all-reduce.6.cloned.1.call-done = f32[32768]{0:T(1024)} async-done(((f32[32768]{0:T(1024)}), f32[32768]{0:T(1024)}) %all-reduce.6.cloned.1.call-update) | async-done | bytes 131088 | tf_op jit(solution)/shard_map/psum | solution.py:114
  344.1 3.3 multiply_bitcast_fusion.1
  347.4 28.2 %while.58 = (s32[]{:T(128)}, f32[18,256]{1,0:T(8,128)S(1)}, f32[8,18,4096]{2,0,1:T(8,128)}, s32[8,4096]{1,0:T(8,128)S(1)}, s32[]{:T(128)}, /*index=5*/s32[]{:T(128)}) while((s32[]{:T(128)}, f32[18,256]{1,0:T(8,128)S(1)}, f32[8,18,4096]{2,0,1:T(8,128)}, s32[8,4096]{1,0:T(8,128)S(1)}, s32[]{:T(128)}, /*index=5*/s32[]{:T(128)}) %tuple.127), condition=%wide.region_13.15_spmd.clone, body=%wide.region_12.14_spmd.clone.sunk | while | flops 227550208 | bytes 970839 | solution.py:50
  375.7 2.3 fusion.27
  377.9 11.3 %all-reduce.2 = (f32[9,2,288]{2,1,0:T(2,128)S(1)}, f32[]{:T(128)}) all-reduce(f32[9,2,288]{2,1,0:T(2,128)S(1)} %fusion.27, f32[]{:T(128)} %get-tuple-element.296), channel_id=1, replica_groups=mesh['obs'=4,'ord'=8] {'obs'}, use_global_device_ids=true, to_apply=%region_14.16 | all-reduce | flops 5185 | bytes 41480 | tf_op jit(solution)/shard_map/psum | solution.py:96
  389.2 30.8 %all_gather.21 = f32[72,2,288]{2,1,0:T(2,128)S(1)} all-gather(f32[9,2,288]{2,1,0:T(2,128)S(1)} %get-tuple-element.292), channel_id=1, replica_groups=mesh['obs'=4,'ord'=8] {'ord'}, dimensions={0}, use_global_device_ids=true | all-gather | bytes 186624 | tf_op jit(solution)/shard_map/all_gather | solution.py:97
  421.9 6.2 multiply_reduce_fusion.2
  428.1 20.1 %psum.68 = f32[]{:T(128)} all-reduce(f32[]{:T(128)} %get-tuple-element.302), channel_id=1, replica_groups=mesh['obs'=4,'ord'=8] {'ord'}, use_global_device_ids=true, to_apply=%region_16.18 | all-reduce | flops 1 | bytes 8 | tf_op jit(solution)/shard_map/psum | solution.py:104
  449.4 30.7 %all_gather.22 = f32[72,2,288]{2,1,0:T(2,128)S(1)} all-gather(f32[9,2,288]{2,1,0:T(2,128)S(1)} %multiply_add_fusion.1), channel_id=1, replica_groups=mesh['obs'=4,'ord'=8] {'ord'}, dimensions={0}, use_global_device_ids=true | all-gather | bytes 186624 | tf_op jit(solution)/shard_map/all_gather | solution.py:112
  483.8 75.9 %while.56 = (s32[]{:T(128)}, f32[8,4096,18]{1,0,2:T(8,128)}, s32[8,4096]{1,0:T(8,128)S(1)}, f32[18,256]{1,0:T(8,128)S(1)}, s32[]{:T(128)}, /*index=5*/s32[]{:T(128)}) while((s32[]{:T(128)}, f32[8,4096,18]{1,0,2:T(8,128)}, s32[8,4096]{1,0:T(8,128)S(1)}, f32[18,256]{1,0:T(8,128)S(1)}, s32[]{:T(128)}, /*index=5*/s32[]{:T(128)}) %tuple.128), condition=%wide.region_18.20_spmd.clone, body=%wide.region_17.19_spmd.clone.sunk | while | flops 227540992 | bytes 1542221 | solution.py:28
  484.1 2.6 convolution_bitcast_fusion.5
  486.9 6.6 dynamic_update_slice.12
  493.5 2.6 convolution_bitcast_fusion.5
  496.4 6.6 dynamic_update_slice.12
  503.0 2.6 convolution_bitcast_fusion.5
  505.9 6.6 dynamic_update_slice.12
  512.5 2.6 convolution_bitcast_fusion.5
  515.3 6.6 dynamic_update_slice.12
  521.9 2.6 convolution_bitcast_fusion.5
  524.8 6.6 dynamic_update_slice.12
  531.4 2.6 convolution_bitcast_fusion.5
  534.3 6.6 dynamic_update_slice.12
  540.8 2.6 convolution_bitcast_fusion.5
  543.7 6.6 dynamic_update_slice.12
  550.3 2.6 convolution_bitcast_fusion.5
  553.2 6.6 dynamic_update_slice.12
  559.8 2.0 pad.8
  564.9 67.5 %all-reduce.8.cloned.1.call-done = f32[32768]{0:T(1024)} async-done(((f32[32768]{0:T(1024)}), f32[32768]{0:T(1024)}) %all-reduce.8.cloned.1.call-update) | async-done | bytes 131088 | tf_op jit(solution)/shard_map/psum | solution.py:114
  634.0 3.3 multiply_bitcast_fusion
  637.4 28.2 %while.59 = (s32[]{:T(128)}, f32[18,256]{1,0:T(8,128)S(1)}, f32[8,18,4096]{2,0,1:T(8,128)}, s32[8,4096]{1,0:T(8,128)S(1)}, s32[]{:T(128)}, /*index=5*/s32[]{:T(128)}) while((s32[]{:T(128)}, f32[18,256]{1,0:T(8,128)S(1)}, f32[8,18,4096]{2,0,1:T(8,128)}, s32[8,4096]{1,0:T(8,128)S(1)}, s32[]{:T(128)}, /*index=5*/s32[]{:T(128)}) %tuple.129), condition=%wide.region_24.26_spmd.clone, body=%wide.region_23.25_spmd.clone.sunk | while | flops 227550208 | bytes 970839 | solution.py:50
  665.6 2.3 fusion.23
  667.9 11.3 %all-reduce.1 = (f32[]{:T(128)}, f32[9,2,288]{2,1,0:T(2,128)S(1)}) all-reduce(f32[]{:T(128)} %get-tuple-element.294, f32[9,2,288]{2,1,0:T(2,128)S(1)} %fusion.23), channel_id=1, replica_groups=mesh['obs'=4,'ord'=8] {'obs'}, use_global_device_ids=true, to_apply=%region_22.24 | all-reduce | flops 5185 | bytes 41480 | tf_op jit(solution)/shard_map/psum | solution.py:116
  679.2 30.8 %all_gather.23 = f32[72,2,288]{2,1,0:T(2,128)S(1)} all-gather(f32[9,2,288]{2,1,0:T(2,128)S(1)} %get-tuple-element.291), channel_id=1, replica_groups=mesh['obs'=4,'ord'=8] {'ord'}, dimensions={0}, use_global_device_ids=true | all-gather | bytes 186624 | tf_op jit(solution)/shard_map/all_gather | solution.py:97
  (171 shorter events, 117.4 us)
Async XLA Ops:
  7.2 101.0 %copy-start = (f32[1,9,288,256]{3,2,1,0:T(8,128)S(1)}, f32[1,9,288,256]{3,2,1,0:T(8,128)}, u32[]{:S(2)}) copy-start(f32[1,9,288,256]{3,2,1,0:T(8,128)} %param.25) | copy-start | bytes 7962628
  7.2 335.4 %all-reduce.6.cloned.1.call-start = ((), (), s32[]{:S(2)}) async-start(), calls=%async_computation | async-start | bytes 262144 | tf_op jit(solution)/shard_map/psum | solution.py:114
  67.2 5.7 copy-start.3
  67.2 6.6 copy-start.4
  67.2 8.0 %copy-start.5 = (s32[1,32768]{1,0:T(1,128)S(1)}, s32[1,32768]{1,0:T(1,128)}, u32[]{:S(2)}) copy-start(s32[1,32768]{1,0:T(1,128)} %param.21) | copy-start | bytes 393220
  270.2 1.9 copy-start.1
  273.5 359.0 %all-reduce.8.cloned.1.call-start = ((), (), s32[]{:S(2)}) async-start(), calls=%async_computation.1 | async-start | bytes 262144 | tf_op jit(solution)/shard_map/psum | solution.py:114
  561.7 1.9 copy-start.2
Sparse Core Ops, SparseCore 0:
  273.6 68.9 all-reduce.5
  565.1 67.3 all-reduce.7
where the time goes:
time: 733 us; the launch traced here: 720 us
  blocking collectives  239 us (33%)
  local copies, waits for them, and re-layouts  183 us (25%)
  waiting for transfers between devices  117 us (16%)
  matrix products  99.8 us (14%)
  other arithmetic  59.5 us (8%)
  between operations  19.7 us (3%)
    psum x2, waiting for transfers between devices, body(): lax.psum(synthesize(coefficients, legendre_here, harmonic, cycle_ids), 'o...  117 us
    dynamic_update_slice x32, local copies, waits for them, and re-layouts, spread_cycles(): pieces = lax.map(one_block, cycle_ids.reshape(blocks, block))  110 us
    all_gather x3, blocking collectives, owner_rows(): everyone = lax.all_gather(summed, 'ord', axis=0, tiled=True)  92.2 us
    all_gather x2, blocking collectives, body(): block_everyone = lax.all_gather(direction, 'ord', axis=0, tiled=True)  61.4 us
    dynamic_slice x64, local copies, waits for them, and re-layouts, collect_cycles(): lax.scan(add_block, jnp.zeros((rows, cycle_count), jnp.float32), (cycle_i...  47 us
    dot_general x16, matrix products, one_block(): jnp.dot(onehot, flat_cycles.T, precision=PRECISE, preferred_element_type=...  40.8 us
    psum x2, blocking collectives, energy(): return lax.psum(jnp.sum(values * precond), 'ord')  39.6 us
    dot_general x24, matrix products, add_block(): jnp.dot(value_block, onehot, precision=PRECISE, preferred_element_type=jn...  36.9 us
  transfers between devices with their start and end apart: 2, of which 2 were waited for; matrix products, arithmetic and copies ran while one was open for 0% of the time, Pallas kernels for 0%

commit v1 on v0

--- a/solution.py
+++ b/solution.py
@@ -111,7 +111,10 @@
     for iteration in range(ITERS):
         block_everyone = lax.all_gather(direction, "ord", axis=0, tiled=True)
         coefficients = jnp.take(block_everyone, slot_of_block, axis=0)
-        gradient = lax.psum(synthesize(coefficients, legendre_here, harmonic, cycle_ids), "ord")
+        gradient = jnp.sum(
+            lax.all_gather(synthesize(coefficients, legendre_here, harmonic, cycle_ids), "ord"),
+            axis=0,
+        )
         weighted = obs_scale * gradient
         curvature_sum = lax.psum(jnp.sum(weighted * gradient), "obs")
         image = owner_rows(adjoint(weighted, legendre_here, harmonic, cycle_ids))

time: 733 us -> 691 us (0.943)
  waiting for transfers between devices: 117 us -> 56.8 us
  matrix products: 99.8 us -> 110 us
    psum x2 -> x0, waiting for transfers between devices: 117 us -> none  [body(): lax.psum(synthesize(coefficients, legendre_here, harmonic, cycle_ids), 'o...]
    all_gather x0 -> x2, waiting for transfers between devices: none -> 56.8 us  [body(): lax.all_gather(synthesize(coefficients, legendre_here, harmonic, cycle_id...]
    dot_general x24, matrix products: 36.9 us -> 46.9 us  [add_block(): jnp.dot(value_block, onehot, precision=PRECISE, preferred_element_type=jn...]
where the time goes in v1:
time: 691 us; the launch traced here: 677 us
  blocking collectives  239 us (35%)
  local copies, waits for them, and re-layouts  189 us (27%)
  matrix products  110 us (16%)
  other arithmetic  61.4 us (9%)
  waiting for transfers between devices  56.8 us (8%)
  between operations  20 us (3%)
    dynamic_update_slice x32, local copies, waits for them, and re-layouts, spread_cycles(): pieces = lax.map(one_block, cycle_ids.reshape(blocks, block))  110 us
    all_gather x3, blocking collectives, owner_rows(): everyone = lax.all_gather(summed, 'ord', axis=0, tiled=True)  92 us
    all_gather x2, blocking collectives, body(): block_everyone = lax.all_gather(direction, 'ord', axis=0, tiled=True)  61.5 us
    all_gather x2, waiting for transfers between devices, body(): lax.all_gather(synthesize(coefficients, legendre_here, harmonic, cycle_id...  56.8 us
    dynamic_slice x64, local copies, waits for them, and re-layouts, collect_cycles(): lax.scan(add_block, jnp.zeros((rows, cycle_count), jnp.float32), (cycle_i...  47 us
    dot_general x24, matrix products, add_block(): jnp.dot(value_block, onehot, precision=PRECISE, preferred_element_type=jn...  46.9 us
    dot_general x16, matrix products, one_block(): jnp.dot(onehot, flat_cycles.T, precision=PRECISE, preferred_element_type=...  40.8 us
    psum x2, blocking collectives, energy(): return lax.psum(jnp.sum(values * precond), 'ord')  39.1 us
  transfers between devices with their start and end apart: 2, of which 2 were waited for; matrix products, arithmetic and copies ran while one was open for 0% of the time, Pallas kernels for 0%

profile of v1, /device:TPU:0, one launch (start us, length us, event | category | flops | bytes accessed | tf_op | source)
XLA Modules:
  0.0 677.5 jit_solution(13195973503372552422)
XLA Ops:
  12.8 13.1 %all-reduce = s32[72]{0:T(128)S(1)} all-reduce(s32[72]{0:T(128)S(1)} %dynamic-update-slice), channel_id=1, replica_groups=mesh['obs'=4,'ord'=8] {'ord'}, use_global_device_ids=true, to_apply=%add | all-reduce | flops 72 | bytes 576
  26.1 33.9 %multiply_cosine_fusion = (f32[9,1,32768]{2,1,0:T(1,128)S(1)}, f32[9,1,32768]{2,1,0:T(1,128)S(1)}) fusion(f32[32768]{0:T(1024)} %bitcast.107, f32[9]{0:T(128)S(1)} %fusion.49), kind=kLoop, calls=%fused_computation.58 | loop fusion | flops 294912 | bytes 2490404 | tf_op jit(solution)/shard_map/cos | solution.py:85
  60.1 3.5 pad_maximum_fusion
  63.5 4.2 stack.10
  67.8 4.6 stack.11
  76.7 3.3 multiply_bitcast_fusion.2
  80.0 28.7 %while.57 = (s32[]{:T(128)}, f32[18,256]{1,0:T(8,128)S(1)}, f32[8,18,4096]{2,0,1:T(8,128)}, s32[8,4096]{1,0:T(8,128)S(1)}, s32[]{:T(128)}, /*index=5*/s32[]{:T(128)}) while((s32[]{:T(128)}, f32[18,256]{1,0:T(8,128)S(1)}, f32[8,18,4096]{2,0,1:T(8,128)}, s32[8,4096]{1,0:T(8,128)S(1)}, s32[]{:T(128)}, /*index=5*/s32[]{:T(128)}) %tuple.105), condition=%wide.region_1.2_spmd.clone, body=%wide.region_0.1_spmd.clone.sunk | while | flops 227550208 | bytes 970839 | solution.py:50
  111.0 10.3 %psum.49 = f32[9,2,288]{2,1,0:T(2,128)S(1)} all-reduce(f32[9,2,288]{2,1,0:T(2,128)S(1)} %fusion.31), channel_id=1, replica_groups=mesh['obs'=4,'ord'=8] {'obs'}, use_global_device_ids=true, to_apply=%region_2.3 | all-reduce | flops 5184 | bytes 41472 | tf_op jit(solution)/shard_map/psum | solution.py:96
  121.3 30.7 %all_gather.30 = f32[72,2,288]{2,1,0:T(2,128)S(1)} all-gather(f32[9,2,288]{2,1,0:T(2,128)S(1)} %psum.49), channel_id=1, replica_groups=mesh['obs'=4,'ord'=8] {'ord'}, dimensions={0}, use_global_device_ids=true | all-gather | bytes 186624 | tf_op jit(solution)/shard_map/all_gather | solution.py:97
  152.6 6.3 multiply_reduce_fusion.1
  158.9 30.7 %all_gather.31 = f32[72,2,288]{2,1,0:T(2,128)S(1)} all-gather(f32[9,2,288]{2,1,0:T(2,128)S(1)} %get-tuple-element.297), channel_id=1, replica_groups=mesh['obs'=4,'ord'=8] {'ord'}, dimensions={0}, use_global_device_ids=true | all-gather | bytes 186624 | tf_op jit(solution)/shard_map/all_gather | solution.py:112
  193.3 75.7 %while.55 = (s32[]{:T(128)}, f32[8,4096,18]{1,0,2:T(8,128)}, s32[8,4096]{1,0:T(8,128)S(1)}, f32[18,256]{1,0:T(8,128)S(1)}, s32[]{:T(128)}, /*index=5*/s32[]{:T(128)}) while((s32[]{:T(128)}, f32[8,4096,18]{1,0,2:T(8,128)}, s32[8,4096]{1,0:T(8,128)S(1)}, f32[18,256]{1,0:T(8,128)S(1)}, s32[]{:T(128)}, /*index=5*/s32[]{:T(128)}) %tuple.124), condition=%wide.region_7.9_spmd.clone, body=%wide.region_6.8_spmd.clone.sunk | while | flops 227540992 | bytes 1542221 | solution.py:28
  193.3 2.6 convolution_bitcast_fusion.4
  196.2 6.6 dynamic_update_slice.11
  202.8 2.6 convolution_bitcast_fusion.4
  205.6 6.6 dynamic_update_slice.11
  212.2 2.6 convolution_bitcast_fusion.4
  215.1 6.6 dynamic_update_slice.11
  221.7 2.6 convolution_bitcast_fusion.4
  224.6 6.6 dynamic_update_slice.11
  231.2 2.6 convolution_bitcast_fusion.4
  234.0 6.6 dynamic_update_slice.11
  240.6 2.6 convolution_bitcast_fusion.4
  243.5 6.6 dynamic_update_slice.11
  250.1 2.6 convolution_bitcast_fusion.4
  253.0 6.6 dynamic_update_slice.11
  259.5 2.6 convolution_bitcast_fusion.4
  262.4 6.6 dynamic_update_slice.11
  274.2 19.3 %psum.50 = f32[]{:T(128)} all-reduce(f32[]{:T(128)} %get-tuple-element.296), channel_id=1, replica_groups=mesh['obs'=4,'ord'=8] {'ord'}, use_global_device_ids=true, to_apply=%region_4.6 | all-reduce | flops 1 | bytes 8 | tf_op jit(solution)/shard_map/psum | solution.py:104
  293.6 19.6 %all-gather.5.cloned.1.call-done = f32[262144]{0:T(1024)} async-done(((f32[32768]{0:T(1024)}), f32[262144]{0:T(1024)}) %all-gather.5.cloned.1.call-update) | async-done | bytes 1048592 | tf_op jit(solution)/shard_map/all_gather | solution.py:115
  317.1 3.3 multiply_bitcast_fusion.1
  320.4 38.1 %while.58 = (s32[]{:T(128)}, f32[18,256]{1,0:T(8,128)}, f32[8,18,4096]{2,0,1:T(8,128)}, s32[8,4096]{1,0:T(8,128)S(1)}, s32[]{:T(128)}, /*index=5*/s32[]{:T(128)}) while((s32[]{:T(128)}, f32[18,256]{1,0:T(8,128)}, f32[8,18,4096]{2,0,1:T(8,128)}, s32[8,4096]{1,0:T(8,128)S(1)}, s32[]{:T(128)}, /*index=5*/s32[]{:T(128)}) %tuple.125), condition=%wide.region_13.15_spmd.clone, body=%wide.region_12.14_spmd.clone.sunk | while | flops 227550208 | bytes 970839 | solution.py:50
  326.5 2.9 fusion.66
  331.4 2.9 fusion.66
  336.2 2.9 fusion.66
  341.1 2.9 fusion.66
  345.9 2.9 fusion.66
  350.8 2.9 fusion.66
  355.6 2.9 fusion.66
  362.2 11.3 %all-reduce.2 = (f32[9,2,288]{2,1,0:T(2,128)S(1)}, f32[]{:T(128)}) all-reduce(f32[9,2,288]{2,1,0:T(2,128)S(1)} %fusion.27, f32[]{:T(128)} %fusion.33), channel_id=1, replica_groups=mesh['obs'=4,'ord'=8] {'obs'}, use_global_device_ids=true, to_apply=%region_14.16 | all-reduce | flops 5185 | bytes 41480 | tf_op jit(solution)/shard_map/psum | solution.py:96
  373.5 30.7 %all_gather.35 = f32[72,2,288]{2,1,0:T(2,128)S(1)} all-gather(f32[9,2,288]{2,1,0:T(2,128)S(1)} %get-tuple-element.292), channel_id=1, replica_groups=mesh['obs'=4,'ord'=8] {'ord'}, dimensions={0}, use_global_device_ids=true | all-gather | bytes 186624 | tf_op jit(solution)/shard_map/all_gather | solution.py:97
  406.2 6.2 multiply_reduce_fusion
  412.4 19.8 %psum.53 = f32[]{:T(128)} all-reduce(f32[]{:T(128)} %get-tuple-element.298), channel_id=1, replica_groups=mesh['obs'=4,'ord'=8] {'ord'}, use_global_device_ids=true, to_apply=%region_16.18 | all-reduce | flops 1 | bytes 8 | tf_op jit(solution)/shard_map/psum | solution.py:104
  433.5 30.8 %all_gather.36 = f32[72,2,288]{2,1,0:T(2,128)S(1)} all-gather(f32[9,2,288]{2,1,0:T(2,128)S(1)} %multiply_add_fusion.1), channel_id=1, replica_groups=mesh['obs'=4,'ord'=8] {'ord'}, dimensions={0}, use_global_device_ids=true | all-gather | bytes 186624 | tf_op jit(solution)/shard_map/all_gather | solution.py:112
  468.0 75.9 %while.56 = (s32[]{:T(128)}, f32[8,4096,18]{1,0,2:T(8,128)}, s32[8,4096]{1,0:T(8,128)S(1)}, f32[18,256]{1,0:T(8,128)S(1)}, s32[]{:T(128)}, /*index=5*/s32[]{:T(128)}) while((s32[]{:T(128)}, f32[8,4096,18]{1,0,2:T(8,128)}, s32[8,4096]{1,0:T(8,128)S(1)}, f32[18,256]{1,0:T(8,128)S(1)}, s32[]{:T(128)}, /*index=5*/s32[]{:T(128)}) %tuple.126), condition=%wide.region_18.20_spmd.clone, body=%wide.region_17.19_spmd.clone.sunk | while | flops 227540992 | bytes 1542221 | solution.py:28
  468.2 2.6 convolution_bitcast_fusion.5
  471.1 6.6 dynamic_update_slice.12
  477.7 2.6 convolution_bitcast_fusion.5
  480.6 6.6 dynamic_update_slice.12
  487.1 2.6 convolution_bitcast_fusion.5
  490.0 6.6 dynamic_update_slice.12
  499.5 6.6 dynamic_update_slice.12
  508.9 6.6 dynamic_update_slice.12
  515.5 2.6 convolution_bitcast_fusion.5
  518.4 6.6 dynamic_update_slice.12
  525.0 2.6 convolution_bitcast_fusion.5
  527.9 6.6 dynamic_update_slice.12
  534.5 2.6 convolution_bitcast_fusion.5
  537.3 6.6 dynamic_update_slice.12
  549.1 37.2 %all-gather.7.cloned.1.call-done = f32[262144]{0:T(1024)} async-done(((f32[32768]{0:T(1024)}), f32[262144]{0:T(1024)}) %all-gather.7.cloned.1.call-update) | async-done | bytes 1048592 | tf_op jit(solution)/shard_map/all_gather | solution.py:115
  590.3 3.3 multiply_bitcast_fusion
  593.6 28.2 %while.59 = (s32[]{:T(128)}, f32[18,256]{1,0:T(8,128)S(1)}, f32[8,18,4096]{2,0,1:T(8,128)}, s32[8,4096]{1,0:T(8,128)S(1)}, s32[]{:T(128)}, /*index=5*/s32[]{:T(128)}) while((s32[]{:T(128)}, f32[18,256]{1,0:T(8,128)S(1)}, f32[8,18,4096]{2,0,1:T(8,128)}, s32[8,4096]{1,0:T(8,128)S(1)}, s32[]{:T(128)}, /*index=5*/s32[]{:T(128)}) %tuple.127), condition=%wide.region_24.26_spmd.clone, body=%wide.region_23.25_spmd.clone.sunk | while | flops 227550208 | bytes 970839 | solution.py:50
  624.9 11.4 %all-reduce.1 = (f32[]{:T(128)}, f32[9,2,288]{2,1,0:T(2,128)S(1)}) all-reduce(f32[]{:T(128)} %fusion.34, f32[9,2,288]{2,1,0:T(2,128)S(1)} %fusion.23), channel_id=1, replica_groups=mesh['obs'=4,'ord'=8] {'obs'}, use_global_device_ids=true, to_apply=%region_22.24 | all-reduce | flops 5185 | bytes 41480 | tf_op jit(solution)/shard_map/psum | solution.py:119
  636.3 30.7 %all_gather.39 = f32[72,2,288]{2,1,0:T(2,128)S(1)} all-gather(f32[9,2,288]{2,1,0:T(2,128)S(1)} %get-tuple-element.291), channel_id=1, replica_groups=mesh['obs'=4,'ord'=8] {'ord'}, dimensions={0}, use_global_device_ids=true | all-gather | bytes 186624 | tf_op jit(solution)/shard_map/all_gather | solution.py:97
  (197 shorter events, 130.7 us)
Async XLA Ops:
  7.2 101.6 %copy-start = (f32[1,9,288,256]{3,2,1,0:T(8,128)S(1)}, f32[1,9,288,256]{3,2,1,0:T(8,128)}, u32[]{:S(2)}) copy-start(f32[1,9,288,256]{3,2,1,0:T(8,128)} %param.25) | copy-start | bytes 7962628
  7.2 306.0 %all-gather.5.cloned.1.call-start = ((), (), s32[]{:S(2)}) async-start(), calls=%async_computation | async-start | bytes 1179648 | tf_op jit(solution)/shard_map/all_gather | solution.py:115
  8.7 143.9 %copy-start.11 = (pred[9]{0:T(512)(128)(4,1)}, pred[9]{0:T(512)(128)(4,1)S(1)}, u32[]{:S(2)}) copy-start(pred[9]{0:T(512)(128)(4,1)S(1)} %compare_and_fusion.1) | copy-start | bytes 31
  26.1 164.0 %copy-start.14 = (pred[9]{0:T(512)(128)(4,1)}, pred[9]{0:T(512)(128)(4,1)S(1)}, u32[]{:S(2)}) copy-start(pred[9]{0:T(512)(128)(4,1)S(1)} %compare_and_fusion) | copy-start | bytes 31
  67.8 5.7 copy-start.3
  67.8 6.6 copy-start.8
  67.8 8.0 %copy-start.9 = (s32[1,32768]{1,0:T(1,128)S(1)}, s32[1,32768]{1,0:T(1,128)}, u32[]{:S(2)}) copy-start(s32[1,32768]{1,0:T(1,128)} %param.21) | copy-start | bytes 393220
  108.7 43.9 %copy-start.6 = (f32[9,288]{1,0:T(8,128)S(1)}, f32[9,288]{1,0:T(8,128)}, u32[]{:S(2)}) copy-start(f32[9,288]{1,0:T(8,128)} %fusion.44) | copy-start | bytes 31108
  152.0 252.2 %copy-start.10 = (s32[1024]{0:T(1024)}, s32[1024]{0:T(1024)S(1)}, u32[]{:S(2)}) copy-start(s32[1024]{0:T(1024)S(1)} %pad_clamp_fusion.1) | copy-start | bytes 12292
  271.0 1.9 copy-start.1
  274.2 312.1 %all-gather.7.cloned.1.call-start = ((), (), s32[]{:S(2)}) async-start(), calls=%async_computation.1 | async-start | bytes 1179648 | tf_op jit(solution)/shard_map/all_gather | solution.py:115
  358.5 47.6 %copy-start.12 = (pred[9]{0:T(512)(128)(4,1)S(1)}, pred[9]{0:T(512)(128)(4,1)}, u32[]{:S(2)}) copy-start(pred[9]{0:T(512)(128)(4,1)} %copy-done.11) | copy-start | bytes 31
  358.5 47.7 %copy-start.7 = (f32[9,288]{1,0:T(8,128)S(1)}, f32[9,288]{1,0:T(8,128)}, u32[]{:S(2)}) copy-start(f32[9,288]{1,0:T(8,128)} %fusion.44) | copy-start | bytes 31108
  361.5 103.3 %copy-start.15 = (pred[9]{0:T(512)(128)(4,1)S(1)}, pred[9]{0:T(512)(128)(4,1)}, u32[]{:S(2)}) copy-start(pred[9]{0:T(512)(128)(4,1)} %copy-done.14) | copy-start | bytes 31
  406.2 60.1 %copy-start.4 = (f32[9,2,288]{2,1,0:T(2,128)}, f32[9,2,288]{2,1,0:T(2,128)S(1)}, u32[]{:S(2)}) copy-start(f32[9,2,288]{2,1,0:T(2,128)S(1)} %fusion.40) | copy-start | bytes 62212
  545.9 1.9 copy-start.2
  621.9 47.8 %copy-start.5 = (f32[9,2,288]{2,1,0:T(2,128)S(1)}, f32[9,2,288]{2,1,0:T(2,128)}, u32[]{:S(2)}) copy-start(f32[9,2,288]{2,1,0:T(2,128)} %copy-done.4) | copy-start | bytes 62212
  621.9 47.8 %copy-start.13 = (pred[9]{0:T(512)(128)(4,1)S(1)}, pred[9]{0:T(512)(128)(4,1)}, u32[]{:S(2)}) copy-start(pred[9]{0:T(512)(128)(4,1)} %copy-done.11) | copy-start | bytes 31
Sparse Core Ops, SparseCore 0:
  274.3 38.8 all-gather.4
  549.2 37.0 all-gather.6
